TPU v7x, 32 devices: a whole 2x2x4 slice. The times are simulated.
32 devices in a mesh: fsdp: 8 (over z, y), ep: 4 (over x, core).
Axes of the slice: x: 2, y: 2, z: 4, core: 2. Of those that a mesh axis runs over, the one named last changes fastest.
Arguments:
- tokens: bfloat16 [4096, 3072], P(('fsdp', 'ep')), may hold values from -6 to 6
- expert_ids: int32 [4096, 2], P(('fsdp', 'ep')), may hold values from 0 to 3, all different within a row; in each aligned block of 128 rows (0 to 127, 128 to 255, ...) at most 128 rows name the same one
- gates: float32 [4096, 2], P(('fsdp', 'ep')), may hold values from 0.2 to 1
- up_weight: bfloat16 [4, 3072, 768], P('ep', 'fsdp'), may hold values from -0.109375 to 0.109375
- down_weight: bfloat16 [4, 768, 3072], P('ep', 'fsdp'), may hold values from -0.21875 to 0.21875
- cotangent: bfloat16 [4096, 3072], P(('fsdp', 'ep')), may hold values from -6 to 6
Outputs:
- mixed: bfloat16 [4096, 3072], P(('fsdp', 'ep'))
- token_grad: bfloat16 [4096, 3072], P(('fsdp', 'ep'))
- up_grad: bfloat16 [4, 3072, 768], P('ep', 'fsdp')
- down_grad: bfloat16 [4, 768, 3072], P('ep', 'fsdp')
Inputs may be any that keep to these rules, and one draw needn't show every extreme that they name: `expert_ids`: each token names two different experts. Among the tokens of one device (aligned blocks of 128 tokens) no expert is named more than 128 times, and in some block one expert is named exactly 128 times.
All inputs are finite; a program needn't handle non-finite values.
Results may differ from a plain program's by a relative error of at most 0.012.
Values may be sent and summed in bfloat16 or wider, within the bound.
A program may use at most 128 MiB of HBM per device.

v0:
```python
import jax
import jax.numpy as jnp
from jax import lax
from jax.sharding import PartitionSpec as P


def gelu_parts(pre):
    root = 0.7978845608028654
    inner = root * (pre + 0.044715 * pre * pre * pre)
    tanh_val = jnp.tanh(inner)
    value = 0.5 * pre * (1.0 + tanh_val)
    slope = 0.5 * (1.0 + tanh_val) + 0.5 * pre * (1.0 - tanh_val * tanh_val) * root * (
        1.0 + 3.0 * 0.044715 * pre * pre
    )
    return (value, slope)


def contract_last(left, right):
    return lax.dot_general(
        left, right, (((1,), (1,)), ((), ())), preferred_element_type=jnp.float32
    )


def contract_first(left, right):
    return lax.dot_general(
        left, right, (((0,), (0,)), ((), ())), preferred_element_type=jnp.float32
    )


def body(tokens, expert_ids, gates, up_weight, down_weight, cotangent):
    n_ep = lax.axis_size("ep")
    tok_count = tokens.shape[0]
    width = tokens.shape[1]
    capacity = 4 * tok_count // n_ep
    slots = n_ep * capacity
    f32 = jnp.float32
    bf16 = jnp.bfloat16
    flat_ids = expert_ids.reshape(-1)
    assigns = flat_ids.shape[0]
    onehot = (flat_ids[:, None] == jnp.arange(n_ep, dtype=jnp.int32)[None, :]).astype(jnp.int32)
    earlier = jnp.cumsum(onehot, axis=0) - onehot
    position = jnp.sum(earlier * onehot, axis=1)
    target = flat_ids * capacity + position
    source = jnp.zeros((slots,), jnp.int32).at[target].set(jnp.arange(assigns, dtype=jnp.int32))
    filled = jnp.zeros((slots,), jnp.bool_).at[target].set(True)
    outgoing = jnp.where(filled[:, None], tokens[source // 2], jnp.zeros((), bf16))
    scaled = (
        (cotangent.astype(f32)[:, None, :] * gates[:, :, None]).astype(bf16).reshape(assigns, width)
    )
    grad_out = jnp.where(filled[:, None], scaled[source], jnp.zeros((), bf16))
    arrived = lax.all_to_all(
        outgoing.reshape(n_ep, capacity, width), "ep", split_axis=0, concat_axis=0, tiled=True
    ).reshape(slots, width)
    columns = arrived
    pre = jnp.dot(
        columns,
        lax.all_gather(up_weight, "fsdp", axis=1, tiled=True)[0],
        preferred_element_type=f32,
    )
    value, slope = gelu_parts(pre)
    hidden = value.astype(bf16)
    columns = hidden
    result = jnp.dot(
        columns,
        lax.all_gather(down_weight, "fsdp", axis=1, tiled=True)[0],
        preferred_element_type=f32,
    )
    expert_out = result.astype(bf16)
    returned = lax.all_to_all(
        expert_out.reshape(n_ep, capacity, width), "ep", split_axis=0, concat_axis=0, tiled=True
    ).reshape(slots, width)
    per_assign = returned[target].astype(f32).reshape(tok_count, 2, width)
    mixed = jnp.sum(per_assign * gates[:, :, None], axis=1).astype(bf16)
    grad_rows = lax.all_to_all(
        grad_out.reshape(n_ep, capacity, width), "ep", split_axis=0, concat_axis=0, tiled=True
    ).reshape(slots, width)
    d_hidden = contract_last(grad_rows, lax.all_gather(down_weight, "fsdp", axis=1, tiled=True)[0])
    d_pre = (d_hidden * slope).astype(bf16)
    back_full = contract_last(d_pre, lax.all_gather(up_weight, "fsdp", axis=1, tiled=True)[0])
    back_rows = back_full.astype(bf16)
    came_back = lax.all_to_all(
        back_rows.reshape(n_ep, capacity, width), "ep", split_axis=0, concat_axis=0, tiled=True
    ).reshape(slots, width)
    token_grad = jnp.sum(came_back[target].astype(f32).reshape(tok_count, 2, width), axis=1).astype(
        bf16
    )
    columns = arrived
    up_grad = lax.psum_scatter(
        contract_first(columns, d_pre).astype(jnp.bfloat16), "fsdp", scatter_dimension=0, tiled=True
    ).astype(jnp.float32)
    columns = hidden
    down_grad = lax.psum_scatter(
        contract_first(columns, grad_rows).astype(jnp.bfloat16),
        "fsdp",
        scatter_dimension=0,
        tiled=True,
    ).astype(jnp.float32)
    return (mixed, token_grad, up_grad.astype(bf16)[None], down_grad.astype(bf16)[None])


def solution(mesh):
    placed = (
        P(("fsdp", "ep"), None),
        P(("fsdp", "ep"), None),
        P(("fsdp", "ep"), None),
        P("ep", "fsdp", None),
        P("ep", "fsdp", None),
        P(("fsdp", "ep"), None),
    )
    return jax.shard_map(
        body,
        mesh=mesh,
        in_specs=placed,
        out_specs=(
            P(("fsdp", "ep"), None),
            P(("fsdp", "ep"), None),
            P("ep", "fsdp", None),
            P("ep", "fsdp", None),
        ),
        check_vma=False,
    )
```

profile of v0, /device:TPU:0, one launch (start us, length us, event | category | flops | bytes accessed | tf_op | source)
XLA Modules:
  0.0 376.8 jit_solution(6498277630989247985)
XLA Ops:
  7.2 0.0 copy-start
  7.2 0.0 copy-start.2
  7.2 0.0 all-gather.3.cloned.1.call-start
  7.2 0.7 all-gather.3.cloned.1.call-update
  7.9 0.0 all-gather.5.cloned.1.call-start
  8.0 0.7 all-gather.5.cloned.1.call-update
  8.7 0.8 copy.14
  9.5 0.1 eq.29
  9.6 0.1 eq.25
  9.8 1.2 reduce-window.6
  11.0 0.1 slice.16
  11.1 0.1 copy.16
  11.2 0.1 copy.17
  11.3 0.7 broadcast_multiply_fusion
  12.0 0.1 copy.13
  12.1 0.1 mul.96
  12.2 0.8 copy.18
  13.0 0.1 mul.109
  13.2 0.0 copy-done.2
  13.2 2.5 mul.107
  15.6 5.2 %mul.108 = f32[256,3072]{1,0:T(8,128)} reshape(f32[128,2,3072]{2,1,0:T(2,128)} %mul.107) | data formatting | bytes 6291456 | tf_op jit(solution)/shard_map/mul | solution.py:48
  20.9 0.1 add_bitcast_fusion
  21.0 1.4 scatter_custom_fusion.1
  22.4 2.2 multiply_convert_fusion
  24.7 3.8 %gather_fusion.2 = bf16[512,3072]{1,0:T(8,128)(2,1)} fusion(bf16[256,3072]{1,0:T(8,128)(2,1)S(1)} %multiply_convert_fusion, s32[1024]{0:T(1024)S(1)} %get-tuple-element.8), kind=kCustom, calls=%fused_computation.2 | custom fusion | bytes 6293504 | tf_op jit(solution)/shard_map/gather | solution.py:50
  28.5 0.0 copy-done
  28.5 3.9 %gather_fusion = bf16[512,3072]{1,0:T(8,128)(2,1)} fusion(bf16[128,3072]{1,0:T(8,128)(2,1)S(1)} %copy-done, s32[1024]{0:T(1024)S(1)} %get-tuple-element.9), kind=kCustom, calls=%fused_computation | custom fusion | bytes 6293504 | tf_op jit(solution)/shard_map/gather | solution.py:46
  32.4 1.5 scatter_custom_fusion
  33.9 5.0 %broadcast_select_fusion = (bf16[4,128,3072]{2,1,0:T(8,128)(2,1)}, bf16[4,128,3072]{2,1,0:T(8,128)(2,1)S(1)}) fusion(bf16[4,128,3072]{2,1,0:T(8,128)(2,1)} %bitcast.55, pred[4,128]{1,0:T(4,128)(4,1)S(1)} %bitcast.66, bf16[4,128,3072]{2,1,0:T(8,128)(2,1)} %bitcast.56), kind=kLoop, calls=%fused_computation.20 | loop fusion | flops 3145728 | bytes 12583424 | tf_op jit(solution)/shard_map/jit(_where)/select_n | solution.py:50
  38.9 41.0 %all_to_all.20 = bf16[4,128,3072]{2,1,0:T(8,128)(2,1)S(1)} all-to-all(bf16[4,128,3072]{2,1,0:T(8,128)(2,1)S(1)} %get-tuple-element.7), channel_id=1, replica_groups=mesh['fsdp'=8,'ep'=4] {'ep'}, dimensions={0} | all-to-all | bytes 6291456 | tf_op jit(solution)/shard_map/all_to_all | solution.py:51
  79.8 4.6 %all-to-all-start.2 = ((bf16[4,128,3072]{2,1,0:T(8,128)(2,1)}), bf16[4,128,3072]{2,1,0:T(8,128)(2,1)}, u32[]{:S(2)}, u32[]{:S(2)}) async-start(bf16[4,128,3072]{2,1,0:T(8,128)(2,1)} %get-tuple-element.6), calls=%async_computation.2 | async-start | bytes 6291456 | tf_op jit(solution)/shard_map/all_to_all | solution.py:74
  84.5 0.2 reduce-scatter.5.cloned.1.call-start
  84.7 8.1 %all-gather.3.cloned.1.call-done = bf16[1,3072,768]{2,1,0:T(8,128)(2,1)} async-done(((bf16[1,384,768]{2,1,0:T(8,128)(2,1)}), bf16[1,3072,768]{2,1,0:T(8,128)(2,1)}) %all-gather.3.cloned.1.call-update) | async-done | bytes 4718608 | tf_op jit(solution)/shard_map/all_gather | solution.py:57
  92.8 6.1 %fusion.6 = f32[512,768]{1,0:T(8,128)} fusion(bf16[512,3072]{1,0:T(8,128)(2,1)S(1)} %bitcast.57, bf16[1,3072,768]{2,1,0:T(8,128)(2,1)} %all-gather.3.cloned.1.call-done), kind=kOutput, calls=%fused_computation.14 | convolution fusion | flops 2415919104 | bytes 9437184 | tf_op jit(solution)/shard_map/dot_general | solution.py:55
  99.0 22.5 %all-to-all-done.2 = bf16[4,128,3072]{2,1,0:T(8,128)(2,1)} async-done(((bf16[4,128,3072]{2,1,0:T(8,128)(2,1)}), bf16[4,128,3072]{2,1,0:T(8,128)(2,1)}, u32[]{:S(2)}, u32[]{:S(2)}) %all-to-all-start.2) | async-done | bytes 3145760 | tf_op jit(solution)/shard_map/all_to_all | solution.py:74
  121.5 7.4 %convolution_convert_fusion = bf16[768,3072]{1,0:T(8,128)(2,1)} fusion(bf16[512,3072]{1,0:T(8,128)(2,1)} %bitcast.12, f32[512,768]{1,0:T(8,128)} %fusion.6), kind=kOutput, calls=%fused_computation.6 | convolution fusion | flops 2421817344 | bytes 9437184 | tf_op jit(solution)/shard_map/dot_general | solution.py:25
  128.9 0.0 reduce-scatter.5.cloned.1.call-update
  128.9 0.0 reduce-scatter.3.cloned.1.call-start
  128.9 44.1 %all-gather.5.cloned.1.call-done = bf16[1,768,3072]{2,1,0:T(8,128)(2,1)} async-done(((bf16[1,96,3072]{2,1,0:T(8,128)(2,1)}), bf16[1,768,3072]{2,1,0:T(8,128)(2,1)}) %all-gather.5.cloned.1.call-update) | async-done | bytes 4718608 | tf_op jit(solution)/shard_map/all_gather | solution.py:65
  173.1 7.0 %fusion.20 = bf16[512,768]{1,0:T(8,128)(2,1)S(1)} fusion(f32[512,768]{1,0:T(8,128)} %fusion.6, bf16[512,3072]{1,0:T(8,128)(2,1)} %bitcast.12, bf16[1,768,3072]{2,1,0:T(8,128)(2,1)} %all-gather.5.cloned.1.call-done), kind=kOutput, calls=%fused_computation.30 | convolution fusion | flops 2423390208 | bytes 10223616 | tf_op jit(solution)/shard_map/dot_general | solution.py:19
  180.1 0.0 copy-start.3
  180.1 0.9 copy-done.3
  181.0 4.3 %convolution_convert_fusion.1 = bf16[3072,768]{1,0:T(8,128)(2,1)} fusion(bf16[512,3072]{1,0:T(8,128)(2,1)S(1)} %bitcast.58, bf16[512,768]{1,0:T(8,128)(2,1)S(1)} %fusion.20), kind=kOutput, calls=%fused_computation.7 | convolution fusion | flops 2418278400 | bytes 8650752 | tf_op jit(solution)/shard_map/dot_general | solution.py:25
  185.3 0.0 copy-start.4
  185.3 0.0 reduce-scatter.3.cloned.1.call-update
  185.3 1.1 copy-done.4
  186.4 6.4 %fusion.8 = bf16[512,3072]{1,0:T(8,128)(2,1)} fusion(bf16[512,768]{1,0:T(8,128)(2,1)S(1)} %copy-done.4, bf16[1,3072,768]{2,1,0:T(8,128)(2,1)} %all-gather.3.cloned.1.call-done), kind=kOutput, calls=%fused_computation.16 | convolution fusion | flops 2417491968 | bytes 8650752 | tf_op jit(solution)/shard_map/dot_general | solution.py:19
  192.8 3.9 %all-to-all-start.3 = ((bf16[4,128,3072]{2,1,0:T(8,128)(2,1)}), bf16[4,128,3072]{2,1,0:T(8,128)(2,1)S(1)}, u32[]{:S(2)}, u32[]{:S(2)}) async-start(bf16[4,128,3072]{2,1,0:T(8,128)(2,1)} %bitcast.60), calls=%async_computation.3 | async-start | bytes 6291456 | tf_op jit(solution)/shard_map/all_to_all | solution.py:81
  196.7 7.3 %fusion.11 = bf16[512,3072]{1,0:T(8,128)(2,1)} fusion(bf16[1,768,3072]{2,1,0:T(8,128)(2,1)} %all-gather.5.cloned.1.call-done, f32[512,768]{1,0:T(8,128)} %fusion.6), kind=kOutput, calls=%fused_computation.17 | convolution fusion | flops 2421030912 | bytes 9437184 | tf_op jit(solution)/shard_map/dot_general | solution.py:63
  204.0 29.6 %all-to-all-done.3 = bf16[4,128,3072]{2,1,0:T(8,128)(2,1)S(1)} async-done(((bf16[4,128,3072]{2,1,0:T(8,128)(2,1)}), bf16[4,128,3072]{2,1,0:T(8,128)(2,1)S(1)}, u32[]{:S(2)}, u32[]{:S(2)}) %all-to-all-start.3) | async-done | bytes 3145760 | tf_op jit(solution)/shard_map/all_to_all | solution.py:81
  233.6 4.6 %all-to-all-start.1 = ((bf16[4,128,3072]{2,1,0:T(8,128)(2,1)}), bf16[4,128,3072]{2,1,0:T(8,128)(2,1)}, u32[]{:S(2)}, u32[]{:S(2)}) async-start(bf16[4,128,3072]{2,1,0:T(8,128)(2,1)} %bitcast.59), calls=%async_computation.1 | async-start | bytes 6291456 | tf_op jit(solution)/shard_map/all_to_all | solution.py:69
  238.3 2.7 gather_fusion.3
  241.0 3.5 gather.24
  244.5 30.8 %all-to-all-done.1 = bf16[4,128,3072]{2,1,0:T(8,128)(2,1)} async-done(((bf16[4,128,3072]{2,1,0:T(8,128)(2,1)}), bf16[4,128,3072]{2,1,0:T(8,128)(2,1)}, u32[]{:S(2)}, u32[]{:S(2)}) %all-to-all-start.1) | async-done | bytes 3145760 | tf_op jit(solution)/shard_map/all_to_all | solution.py:69
  275.3 6.6 %gather_fusion.1 = bf16[256,3072]{1,0:T(8,128)(2,1)} fusion(bf16[512,3072]{1,0:T(8,128)(2,1)} %bitcast.10, s32[1024]{0:T(1024)S(1)} %pad_clamp_fusion.1), kind=kCustom, calls=%fused_computation.1 | custom fusion | bytes 3146752 | tf_op jit(solution)/shard_map/gather | solution.py:72
  281.8 5.1 %reshape.104 = f32[128,2,3072]{2,1,0:T(2,128)} reshape(bf16[256,3072]{1,0:T(8,128)(2,1)} %gather_fusion.1) | data formatting | bytes 4718592 | tf_op jit(solution)/shard_map/convert_element_type | solution.py:72
  286.9 0.0 copy-start.1
  286.9 5.1 %reduce_sum.35 = bf16[128,3072]{1,0:T(8,128)(2,1)} reduce(bf16[128,2,3072]{2,1,0:T(2,128)(2,1)S(1)} %gather.24, bf16[]{:T(256)} %constant.14.clone.1), dimensions={1}, to_apply=%region_6.7 | reduce | flops 393216 | bytes 2359298 | tf_op jit(solution)/shard_map/reduce_sum | solution.py:84
  292.0 7.3 %multiply_reduce_fusion = bf16[128,3072]{1,0:T(8,128)(2,1)} fusion(f32[128,2,3072]{2,1,0:T(2,128)} %reshape.104, f32[128,2]{1,0:T(8,128)S(1)} %copy.18), kind=kLoop, calls=%fused_computation.19 | loop fusion | flops 1179648 | bytes 3933184 | tf_op jit(solution)/shard_map/reduce_sum | solution.py:73
  299.3 0.0 reduce-scatter.5.cloned.1.call-done
  299.3 70.5 %reduce-scatter.3.cloned.1.call-done = bf16[384,768]{1,0:T(8,128)(2,1)} async-done(((bf16[3072,768]{1,0:T(8,128)(2,1)}), bf16[384,768]{1,0:T(8,128)(2,1)}) %reduce-scatter.3.cloned.1.call-update) | async-done | bytes 589840 | tf_op jit(solution)/shard_map/reduce_scatter | solution.py:88
  369.8 0.0 copy-done.1
  (10 shorter events, 0.1 us)
Async XLA Ops:
  7.2 21.3 %copy-start = (bf16[128,3072]{1,0:T(8,128)(2,1)S(1)}, bf16[128,3072]{1,0:T(8,128)(2,1)}, u32[]{:S(2)}) copy-start(bf16[128,3072]{1,0:T(8,128)(2,1)} %param.6) | copy-start | bytes 2359300
  7.2 6.0 %copy-start.2 = (bf16[128,3072]{1,0:T(8,128)(2,1)S(1)}, bf16[128,3072]{1,0:T(8,128)(2,1)}, u32[]{:S(2)}) copy-start(bf16[128,3072]{1,0:T(8,128)(2,1)} %param.11) | copy-start | bytes 2359300
  7.2 85.6 %all-gather.3.cloned.1.call-start = ((), (), s32[]{:S(2)}) async-start(), calls=%async_computation.6 | async-start | bytes 5308416 | tf_op jit(solution)/shard_map/all_gather | solution.py:57
  7.9 165.1 %all-gather.5.cloned.1.call-start = ((), (), s32[]{:S(2)}) async-start(), calls=%async_computation.7 | async-start | bytes 5308416 | tf_op jit(solution)/shard_map/all_gather | solution.py:65
  79.8 41.6 %all-to-all-start.2 = ((bf16[4,128,3072]{2,1,0:T(8,128)(2,1)}), bf16[4,128,3072]{2,1,0:T(8,128)(2,1)}, u32[]{:S(2)}, u32[]{:S(2)}) async-start(bf16[4,128,3072]{2,1,0:T(8,128)(2,1)} %get-tuple-element.6), calls=%async_computation.2 | async-start | bytes 6291456 | tf_op jit(solution)/shard_map/all_to_all | solution.py:74
  84.5 214.8 %reduce-scatter.5.cloned.1.call-start = ((), (), s32[]{:S(2)}) async-start(), calls=%async_computation.9 | async-start | bytes 5308416 | tf_op jit(solution)/shard_map/reduce_scatter | solution.py:92
  128.9 240.9 %reduce-scatter.3.cloned.1.call-start = ((), (), s32[]{:S(2)}) async-start(), calls=%async_computation.8 | async-start | bytes 5308416 | tf_op jit(solution)/shard_map/reduce_scatter | solution.py:88
  180.1 0.9 copy-start.3
  185.3 1.1 copy-start.4
  192.8 40.8 %all-to-all-start.3 = ((bf16[4,128,3072]{2,1,0:T(8,128)(2,1)}), bf16[4,128,3072]{2,1,0:T(8,128)(2,1)S(1)}, u32[]{:S(2)}, u32[]{:S(2)}) async-start(bf16[4,128,3072]{2,1,0:T(8,128)(2,1)} %bitcast.60), calls=%async_computation.3 | async-start | bytes 6291456 | tf_op jit(solution)/shard_map/all_to_all | solution.py:81
  233.6 41.6 %all-to-all-start.1 = ((bf16[4,128,3072]{2,1,0:T(8,128)(2,1)}), bf16[4,128,3072]{2,1,0:T(8,128)(2,1)}, u32[]{:S(2)}, u32[]{:S(2)}) async-start(bf16[4,128,3072]{2,1,0:T(8,128)(2,1)} %bitcast.59), calls=%async_computation.1 | async-start | bytes 6291456 | tf_op jit(solution)/shard_map/all_to_all | solution.py:69
  286.9 82.9 %copy-start.1 = (bf16[128,3072]{1,0:T(8,128)(2,1)S(1)}, bf16[128,3072]{1,0:T(8,128)(2,1)}, u32[]{:S(2)}) copy-start(bf16[128,3072]{1,0:T(8,128)(2,1)} %param.6) | copy-start | bytes 2359300
Sparse Core Ops, SparseCore 0:
  10.2 82.5 all-gather.2
  95.0 78.0 all-gather.4
  177.3 93.3 reduce-scatter.4
  274.8 94.9 reduce-scatter.2
where the time goes:
time: 384 us; the launch traced here: 377 us
  waiting for transfers between devices  207 us (54%)
  blocking collectives  41 us (11%)
  local copies, waits for them, and re-layouts  40.6 us (11%)
  matrix products  38.6 us (10%)
  other arithmetic  21.7 us (6%)
  between operations  14.4 us (4%)
  starting transfers between devices  13.5 us (4%)
    reduce_scatter x1, waiting for transfers between devices, body(): lax.psum_scatter(contract_first(columns, d_pre).astype(jnp.bfloat16), 'fs...  70.5 us
    all_gather x1, waiting for transfers between devices, body(): lax.all_gather(down_weight, 'fsdp', axis=1, tiled=True)[0]  44.1 us
    all_to_all x1, blocking collectives, body(): lax.all_to_all(outgoing.reshape(n_ep, capacity, width), 'ep', split_axis=...  41 us
    all_to_all x1, waiting for transfers between devices, body(): lax.all_to_all(expert_out.reshape(n_ep, capacity, width), 'ep', split_axi...  30.8 us
    all_to_all x1, waiting for transfers between devices, body(): lax.all_to_all(back_rows.reshape(n_ep, capacity, width), 'ep', split_axis...  29.6 us
    all_to_all x1, waiting for transfers between devices, body(): lax.all_to_all(grad_out.reshape(n_ep, capacity, width), 'ep', split_axis=...  22.5 us
    dot_general x2, matrix products, contract_last(): lax.dot_general(left, right, (((1,), (1,)), ((), ())), preferred_element_...  13.4 us
    dot_general x2, matrix products, contract_first(): lax.dot_general(left, right, (((0,), (0,)), ((), ())), preferred_element_...  11.7 us
  transfers between devices with their start and end apart: 7, of which 6 were waited for; matrix products, arithmetic and copies ran while one was open for 26% of the time, Pallas kernels for 0%

commit v1 on v0

v1 whole, which is shorter than its diff:
```python
import jax
import jax.numpy as jnp
from jax import lax
from jax.sharding import PartitionSpec as P


def gelu_parts(pre):
    root = 0.7978845608028654
    inner = root * (pre + 0.044715 * pre * pre * pre)
    tanh_val = jnp.tanh(inner)
    value = 0.5 * pre * (1.0 + tanh_val)
    slope = 0.5 * (1.0 + tanh_val) + 0.5 * pre * (1.0 - tanh_val * tanh_val) * root * (
        1.0 + 3.0 * 0.044715 * pre * pre
    )
    return (value, slope)


def contract_last(left, right):
    return lax.dot_general(
        left, right, (((1,), (1,)), ((), ())), preferred_element_type=jnp.float32
    )


def contract_first(left, right):
    return lax.dot_general(
        left, right, (((0,), (0,)), ((), ())), preferred_element_type=jnp.float32
    )


def body(tokens, expert_ids, gates, up_weight, down_weight, cotangent):
    n_ep = lax.axis_size("ep")
    f32 = jnp.float32
    bf16 = jnp.bfloat16
    chosen = expert_ids[:, :, None] == jnp.arange(n_ep, dtype=jnp.int32)[None, None, :]
    dense_gates = jnp.sum(jnp.where(chosen, gates[:, :, None], 0.0), axis=1)
    all_gates = lax.all_gather(dense_gates, "ep", axis=0, tiled=True)
    mine = lax.axis_index("ep") == jnp.arange(n_ep, dtype=jnp.int32)
    gate = jnp.sum(jnp.where(mine[None, :], all_gates, 0.0), axis=1, keepdims=True)
    rows = lax.all_gather(tokens, "ep", axis=0, tiled=True)
    up = lax.all_gather(up_weight, "fsdp", axis=1, tiled=True)[0]
    cot = lax.all_gather(cotangent, "ep", axis=0, tiled=True)
    down = lax.all_gather(down_weight, "fsdp", axis=1, tiled=True)[0]
    grad_rows = (cot.astype(f32) * gate).astype(bf16)
    pre = jnp.dot(rows, up, preferred_element_type=f32)
    value, slope = gelu_parts(pre)
    hidden = value.astype(bf16)
    down_grad = lax.psum_scatter(
        contract_first(hidden, grad_rows).astype(bf16), "fsdp", scatter_dimension=0, tiled=True
    )
    d_hidden = contract_last(grad_rows, down)
    d_pre = (d_hidden * slope).astype(bf16)
    up_grad = lax.psum_scatter(
        contract_first(rows, d_pre).astype(bf16), "fsdp", scatter_dimension=0, tiled=True
    )
    result = jnp.dot(hidden, down, preferred_element_type=f32)
    mixed = lax.psum_scatter((result * gate).astype(bf16), "ep", scatter_dimension=0, tiled=True)
    back = contract_last(d_pre, up).astype(bf16)
    token_grad = lax.psum_scatter(back, "ep", scatter_dimension=0, tiled=True)
    return (mixed, token_grad, up_grad[None], down_grad[None])


def solution(mesh):
    placed = (
        P(("fsdp", "ep"), None),
        P(("fsdp", "ep"), None),
        P(("fsdp", "ep"), None),
        P("ep", "fsdp", None),
        P("ep", "fsdp", None),
        P(("fsdp", "ep"), None),
    )
    return jax.shard_map(
        body,
        mesh=mesh,
        in_specs=placed,
        out_specs=(
            P(("fsdp", "ep"), None),
            P(("fsdp", "ep"), None),
            P("ep", "fsdp", None),
            P("ep", "fsdp", None),
        ),
        check_vma=False,
    )
```

time: 384 us -> 535 us (1.39); the launches traced: 377 us -> 534 us
  waiting for transfers between devices: 207 us -> 461 us
  blocking collectives: 41 us -> 6.11 us
  local copies, waits for them, and re-layouts: 40.6 us -> 14.3 us
  other arithmetic: 21.7 us -> 0.11 us
  starting transfers between devices: 13.5 us -> 0.31 us
    all_gather x2 -> x4, waiting for transfers between devices: 52.3 us -> 210 us  [the longest x1 82.1 us: body(): up = lax.all_gather(up_weight, 'fsdp', axis=1, tiled=True)[0]]
    reduce_scatter x2 -> x3, waiting for transfers between devices: 70.5 us -> 179 us  [the longest x1 99.7 us: body(): lax.psum_scatter(contract_first(hidden, grad_rows).astype(bf16), 'fsdp',...]
    all_to_all x3 -> x0, waiting for transfers between devices: 82.8 us -> none  [the longest x1 30.8 us: body(): lax.all_to_all(expert_out.reshape(n_ep, capacity, width), 'ep', split_axi...]
    unnamed x4 -> x9, waiting for transfers between devices: 1.41 us -> 72.4 us
    all_to_all x1 -> x0, blocking collectives: 41 us -> none  [body(): lax.all_to_all(outgoing.reshape(n_ep, capacity, width), 'ep', split_axis=...]
    gather x5 -> x0, local copies, waits for them, and re-layouts: 20.5 us -> none  [the longest x1 6.59 us: body(): per_assign = returned[target].astype(f32).reshape(tok_count, 2, width)]
    all_to_all x3 -> x0, starting transfers between devices: 13.2 us -> none  [the longest x1 4.64 us: body(): lax.all_to_all(expert_out.reshape(n_ep, capacity, width), 'ep', split_axi...]
    reduce_sum x3 -> x2, other arithmetic: 12.4 us -> 0.1 us  [the longest x1 0.09 us: body(): jnp.sum(jnp.where(mine[None, :], all_gates, 0.0), axis=1, keepdims=True)]
  transfers between devices with their start and end apart: 7 -> 8, of which waited for: 6 -> 8; matrix products, arithmetic and copies ran while one was open for 26% -> 5% of each run, Pallas kernels for 0% -> 0%
where the time goes in v1:
time: 535 us; the launch traced here: 534 us
  waiting for transfers between devices  461 us (86%)
  matrix products  37.8 us (7%)
  local copies, waits for them, and re-layouts  14.3 us (3%)
  between operations  14.2 us (3%)
  blocking collectives  6.11 us (1%)
    reduce_scatter x1, waiting for transfers between devices, body(): lax.psum_scatter(contract_first(hidden, grad_rows).astype(bf16), 'fsdp',...  99.7 us
    all_gather x1, waiting for transfers between devices, body(): up = lax.all_gather(up_weight, 'fsdp', axis=1, tiled=True)[0]  82.1 us
    all_gather x1, waiting for transfers between devices, body(): down = lax.all_gather(down_weight, 'fsdp', axis=1, tiled=True)[0]  82 us
    unnamed x9, waiting for transfers between devices  72.4 us
    reduce_scatter x1, waiting for transfers between devices, body(): token_grad = lax.psum_scatter(back, 'ep', scatter_dimension=0, tiled=True)  41.2 us
    reduce_scatter x1, waiting for transfers between devices, body(): lax.psum_scatter((result * gate).astype(bf16), 'ep', scatter_dimension=0,...  38.3 us
    all_gather x1, waiting for transfers between devices, body(): rows = lax.all_gather(tokens, 'ep', axis=0, tiled=True)  24.6 us
    all_gather x1, waiting for transfers between devices, body(): cot = lax.all_gather(cotangent, 'ep', axis=0, tiled=True)  21.2 us
  transfers between devices with their start and end apart: 8, of which 8 were waited for; matrix products, arithmetic and copies ran while one was open for 5% of the time, Pallas kernels for 0%

profile of v1, /device:TPU:0, one launch (start us, length us, event | category | flops | bytes accessed | tf_op | source)
XLA Modules:
  0.0 534.1 jit_solution(15591842795536665031)
XLA Ops:
  7.2 0.0 copy-start
  7.2 0.0 copy-start.1
  7.2 0.0 all-gather.5.cloned.1.call-start
  7.2 0.7 all-gather.5.cloned.1.call-update
  7.9 0.0 all-gather.7.cloned.1.call-start
  8.0 0.7 all-gather.7.cloned.1.call-update
  8.7 0.0 all-gather.11.cloned.1.call-start
  8.7 0.7 all-gather.11.cloned.1.call-update
  9.4 0.0 all-gather.9.cloned.1.call-start
  9.5 0.5 all-gather.9.cloned.1.call-update
  10.0 0.0 reduce-scatter.13.cloned.1.call-start
  10.0 0.0 copy-done
  10.0 0.0 copy-done.1
  10.1 6.1 %all_gather.18 = f32[512,4]{0,1:T(4,128)S(1)} all-gather(f32[128,4]{0,1:T(4,128)S(1)} %select_reduce_fusion.1), channel_id=1, replica_groups=mesh['fsdp'=8,'ep'=4] {'ep'}, dimensions={0}, use_global_device_ids=true | all-gather | bytes 10240 | tf_op jit(solution)/shard_map/all_gather | solution.py:36
  16.2 0.1 select_reduce_fusion
  16.3 24.6 %all-gather.5.cloned.1.call-done = bf16[512,3072]{1,0:T(8,128)(2,1)} async-done(((bf16[128,3072]{1,0:T(8,128)(2,1)}), bf16[512,3072]{1,0:T(8,128)(2,1)}) %all-gather.5.cloned.1.call-update) | async-done | bytes 3145744 | tf_op jit(solution)/shard_map/all_gather | solution.py:39
  40.8 82.1 %all-gather.7.cloned.1.call-done = bf16[1,3072,768]{2,1,0:T(8,128)(2,1)} async-done(((bf16[1,384,768]{2,1,0:T(8,128)(2,1)}), bf16[1,3072,768]{2,1,0:T(8,128)(2,1)}) %all-gather.7.cloned.1.call-update) | async-done | bytes 4718608 | tf_op jit(solution)/shard_map/all_gather | solution.py:40
  122.9 7.1 %fusion.5 = f32[512,768]{1,0:T(8,128)} fusion(bf16[512,3072]{1,0:T(8,128)(2,1)} %all-gather.5.cloned.1.call-done, bf16[1,3072,768]{2,1,0:T(8,128)(2,1)} %all-gather.7.cloned.1.call-done), kind=kOutput, calls=%fused_computation.9 | convolution fusion | flops 2415919104 | bytes 9437184 | tf_op jit(solution)/shard_map/dot_general | solution.py:44
  130.0 0.0 copy-start.3
  130.0 21.2 %all-gather.11.cloned.1.call-done = bf16[512,3072]{1,0:T(8,128)(2,1)} async-done(((bf16[128,3072]{1,0:T(8,128)(2,1)}), bf16[512,3072]{1,0:T(8,128)(2,1)}) %all-gather.11.cloned.1.call-update) | async-done | bytes 3145744 | tf_op jit(solution)/shard_map/all_gather | solution.py:41
  151.2 82.0 %all-gather.9.cloned.1.call-done = bf16[1,768,3072]{2,1,0:T(8,128)(2,1)} async-done(((bf16[1,96,3072]{2,1,0:T(8,128)(2,1)}), bf16[1,768,3072]{2,1,0:T(8,128)(2,1)}) %all-gather.9.cloned.1.call-update) | async-done | bytes 4718608 | tf_op jit(solution)/shard_map/all_gather | solution.py:42
  233.2 7.0 %fusion.17 = bf16[512,768]{1,0:T(8,128)(2,1)S(1)} fusion(f32[512,768]{1,0:T(8,128)} %fusion.5, bf16[1,768,3072]{2,1,0:T(8,128)(2,1)} %all-gather.9.cloned.1.call-done, bf16[512,3072]{1,0:T(8,128)(2,1)} %all-gather.11.cloned.1.call-done, f32[512]{0:T(512)S(1)} %select_reduce_fusion), kind=kOutput, calls=%fused_computation.21 | convolution fusion | flops 2428108800 | bytes 10225664 | tf_op jit(solution)/shard_map/dot_general | solution.py:19
  240.2 0.0 copy-start.5
  240.2 0.9 copy-done.5
  241.1 0.0 copy-done.3
  241.1 4.3 fusion.7
  245.4 6.7 %copy.17 = bf16[3072,768]{1,0:T(8,128)(2,1)} copy(bf16[3072,768]{0,1:T(8,128)(2,1)} %fusion.7) | data formatting | bytes 9437184
  252.1 0.0 copy-start.4
  252.1 0.0 reduce-scatter.13.cloned.1.call-update
  252.2 0.0 reduce-scatter.7.cloned.1.call-start
  252.2 1.3 copy-done.4
  253.6 6.5 %multiply_convert_fusion.1 = bf16[512,3072]{1,0:T(8,128)(2,1)} fusion(bf16[1,768,3072]{2,1,0:T(8,128)(2,1)} %all-gather.9.cloned.1.call-done, f32[512]{0:T(512)S(1)} %select_reduce_fusion, f32[512,768]{1,0:T(8,128)S(1)} %copy-done.4), kind=kOutput, calls=%fused_computation.1 | convolution fusion | flops 2422603776 | bytes 9439232 | tf_op jit(solution)/shard_map/dot_general | solution.py:55
  260.0 0.0 copy-start.6
  260.0 0.0 reduce-scatter.7.cloned.1.call-update
  260.0 0.0 reduce-scatter.9.cloned.1.call-start
  260.1 1.1 copy-done.6
  261.1 6.4 %fusion.8 = bf16[512,3072]{1,0:T(8,128)(2,1)} fusion(bf16[512,768]{1,0:T(8,128)(2,1)S(1)} %copy-done.6, bf16[1,3072,768]{2,1,0:T(8,128)(2,1)} %all-gather.7.cloned.1.call-done), kind=kOutput, calls=%fused_computation.12 | convolution fusion | flops 2417491968 | bytes 8650752 | tf_op jit(solution)/shard_map/dot_general | solution.py:19
  267.5 0.0 copy-start.2
  267.5 0.0 reduce-scatter.9.cloned.1.call-update
  267.6 0.0 reduce-scatter.11.cloned.1.call-start
  267.6 1.8 copy-done.2
  269.5 6.5 %convolution_convert_fusion = bf16[768,3072]{1,0:T(8,128)(2,1)} fusion(bf16[512,3072]{1,0:T(8,128)(2,1)S(1)} %copy-done.2, f32[512]{0:T(512)S(1)} %select_reduce_fusion, f32[512,768]{1,0:T(8,128)} %fusion.5), kind=kOutput, calls=%fused_computation.2 | convolution fusion | flops 2426535936 | bytes 9439232 | tf_op jit(solution)/shard_map/dot_general | solution.py:25
  275.9 0.0 reduce-scatter.11.cloned.1.call-update
  276.0 69.8 %reduce-scatter.13.cloned.1.call-done = bf16[384,768]{1,0:T(8,128)(2,1)} async-done(((bf16[3072,768]{1,0:T(8,128)(2,1)}), bf16[384,768]{1,0:T(8,128)(2,1)}) %reduce-scatter.13.cloned.1.call-update) | async-done | bytes 589840
  345.7 1.4 copy.18
  347.1 1.1 copy.16
  348.2 38.3 %reduce-scatter.7.cloned.1.call-done = bf16[128,3072]{1,0:T(8,128)(2,1)} async-done(((bf16[512,3072]{1,0:T(8,128)(2,1)}), bf16[128,3072]{1,0:T(8,128)(2,1)}) %reduce-scatter.7.cloned.1.call-update) | async-done | bytes 786448 | tf_op jit(solution)/shard_map/reduce_scatter | solution.py:56
  386.4 41.2 %reduce-scatter.9.cloned.1.call-done = bf16[128,3072]{1,0:T(8,128)(2,1)} async-done(((bf16[512,3072]{1,0:T(8,128)(2,1)}), bf16[128,3072]{1,0:T(8,128)(2,1)}) %reduce-scatter.9.cloned.1.call-update) | async-done | bytes 786448 | tf_op jit(solution)/shard_map/reduce_scatter | solution.py:58
  427.6 99.7 %reduce-scatter.11.cloned.1.call-done = bf16[96,3072]{1,0:T(8,128)(2,1)} async-done(((bf16[768,3072]{1,0:T(8,128)(2,1)}), bf16[96,3072]{1,0:T(8,128)(2,1)}) %reduce-scatter.11.cloned.1.call-update) | async-done | bytes 589840 | tf_op jit(solution)/shard_map/reduce_scatter | solution.py:47
  (2 shorter events, 0.0 us)
Async XLA Ops:
  7.2 2.9 copy-start
  7.2 2.9 copy-start.1
  7.2 33.7 %all-gather.5.cloned.1.call-start = ((), (), s32[]{:S(2)}) async-start(), calls=%async_computation.4 | async-start | bytes 3932160 | tf_op jit(solution)/shard_map/all_gather | solution.py:39
  7.9 115.0 %all-gather.7.cloned.1.call-start = ((), (), s32[]{:S(2)}) async-start(), calls=%async_computation.5 | async-start | bytes 5308416 | tf_op jit(solution)/shard_map/all_gather | solution.py:40
  8.7 142.5 %all-gather.11.cloned.1.call-start = ((), (), s32[]{:S(2)}) async-start(), calls=%async_computation.8 | async-start | bytes 3932160 | tf_op jit(solution)/shard_map/all_gather | solution.py:41
  9.4 223.8 %all-gather.9.cloned.1.call-start = ((), (), s32[]{:S(2)}) async-start(), calls=%async_computation.6 | async-start | bytes 5308416 | tf_op jit(solution)/shard_map/all_gather | solution.py:42
  10.0 335.7 %reduce-scatter.13.cloned.1.call-start = ((), (), s32[]{:S(2)}) async-start(), calls=%async_computation.11 | async-start | bytes 5308416
  130.0 111.0 %copy-start.3 = (bf16[512,3072]{1,0:T(8,128)(2,1)S(1)}, bf16[512,3072]{1,0:T(8,128)(2,1)}, u32[]{:S(2)}) copy-start(bf16[512,3072]{1,0:T(8,128)(2,1)} %all-gather.5.cloned.1.call-done) | copy-start | bytes 9437188
  240.2 0.9 copy-start.5
  252.1 1.4 copy-start.4
  252.2 134.2 %reduce-scatter.7.cloned.1.call-start = ((), (), s32[]{:S(2)}) async-start(), calls=%async_computation.7 | async-start | bytes 3932160 | tf_op jit(solution)/shard_map/reduce_scatter | solution.py:56
  260.0 1.1 copy-start.6
  260.0 167.6 %reduce-scatter.9.cloned.1.call-start = ((), (), s32[]{:S(2)}) async-start(), calls=%async_computation.9 | async-start | bytes 3932160 | tf_op jit(solution)/shard_map/reduce_scatter | solution.py:58
  267.5 1.9 copy-start.2
  267.6 259.7 %reduce-scatter.11.cloned.1.call-start = ((), (), s32[]{:S(2)}) async-start(), calls=%async_computation.10 | async-start | bytes 5308416 | tf_op jit(solution)/shard_map/reduce_scatter | solution.py:47
Sparse Core Ops, SparseCore 0:
  9.6 31.2 all-gather.4
  43.0 79.8 all-gather.6
  124.5 26.6 all-gather.10
  153.3 79.8 all-gather.8
  252.3 93.3 reduce-scatter.12
  348.7 37.6 reduce-scatter.6
  389.7 37.9 reduce-scatter.8
  431.9 95.3 reduce-scatter.10

commit v2 on v1

v2 whole, which is shorter than its diff:
```python
import functools

import jax
import jax.numpy as jnp
from jax import lax
from jax.experimental import pallas as pl
from jax.experimental.pallas import tpu as pltpu
from jax.sharding import PartitionSpec as P

F32 = jnp.float32
BF16 = jnp.bfloat16
MESH = pl.DeviceIdType.MESH
LANES = 128


def gelu_parts(pre):
    root = 0.7978845608028654
    inner = root * (pre + 0.044715 * pre * pre * pre)
    tanh_val = jnp.tanh(inner)
    value = 0.5 * pre * (1.0 + tanh_val)
    slope = 0.5 * (1.0 + tanh_val) + 0.5 * pre * (1.0 - tanh_val * tanh_val) * root * (
        1.0 + 3.0 * 0.044715 * pre * pre
    )
    return (value, slope)


def dot(left, right, dims):
    return lax.dot_general(left, right, (dims, ((), ())), preferred_element_type=F32)


NN = ((1,), (0,))
NT = ((1,), (1,))
TN = ((0,), (0,))


def tiles(count, size):
    def run(fn):
        @pl.loop(0, count // size)
        def _(i):
            fn(pl.ds(pl.multiple_of(i * size, size), size))

    return run


def kernel(
    nz, ny, nx,
    tok_in, cot_in, gate_in, up_in, down_in,
    mixed_out, tg_out, ug_out, dg_out,
    up, down, tok, cot, gate, slope, hidden, dpre, upart, dpart,
    ry_u, ry_d, rz_u, rz_d, rc_m, rc_t, rx_m, rx_t,
    local_sem, wz_s, wz_r, wy_s, wy_r, tx_s, tx_r, tc_s, tc_r, g_s, g_r,
    ry_s, ry_r, rz_s, rz_r, rc_s, rc_r, rx_s, rx_r,
):
    ne = 2 * nx
    f = lax.axis_index("fsdp")
    e = lax.axis_index("ep")
    z, y = lax.div(f, ny), lax.rem(f, ny)
    x, c = lax.div(e, 2), lax.rem(e, 2)
    T = tok_in.shape[0]
    D = tok_in.shape[1]
    R = ne * T
    FF = up.shape[1]

    def zp(k):
        return lax.rem(z + k + nz, nz)

    def yp(j):
        return lax.rem(y + j + ny, ny)

    def xp(k):
        return lax.rem(x + k + nx, nx)

    def fdev(zz, yy):
        return {"fsdp": zz * ny + yy}

    def edev(xx, cc):
        return {"ep": xx * 2 + cc}

    def rows(ref, index, size):
        return ref.at[pl.ds(pl.multiple_of(index * size, size), size)]

    def remote(src, dst, ss, rs, dev):
        return pltpu.make_async_remote_copy(
            src_ref=src, dst_ref=dst, send_sem=ss, recv_sem=rs,
            device_id=dev, device_id_type=MESH,
        )

    sends = []

    def send(src, dst, ss, rs, dev):
        copy = remote(src, dst, ss, rs, dev)
        copy.start()
        sends.append(copy)
        return copy

    barrier = pltpu.get_barrier_semaphore()
    peers = [fdev(zp(k), y) for k in range(1, nz)]
    peers += [fdev(z, yp(j)) for j in range(1, ny)]
    peers += [{"ep": lax.rem(e + i, ne)} for i in range(1, ne)]
    for dev in peers:
        pl.semaphore_signal(barrier, inc=1, device_id=dev, device_id_type=MESH)
    locals_ = []
    for i, (src, dst) in enumerate((
        (up_in.at[0], rows(up, f, up_in.shape[1])),
        (down_in.at[0], rows(down, f, down_in.shape[1])),
        (tok_in, rows(tok, e, T)),
        (cot_in, rows(cot, e, T)),
    )):
        copy = pltpu.make_async_copy(src, dst, local_sem.at[i])
        copy.start()
        locals_.append(copy)
    rows(gate, e, T)[...] = gate_in[e]
    pl.semaphore_wait(barrier, len(peers))

    weights = ((up_in, up), (down_in, down))
    zorder = [1, nz - 1] + list(range(2, nz - 1))

    def weight_start(w):
        src, full = weights[w]
        size = src.shape[1]
        for k in zorder:
            send(src.at[0], rows(full, f, size), wz_s.at[w, k - 1], wz_r.at[w, k - 1],
                 fdev(zp(k), y))
        for j in range(1, ny):
            send(src.at[0], rows(full, f, size), wy_s.at[w, 0, j - 1], wy_r.at[w, 0, j - 1],
                 fdev(z, yp(j)))

    def weight_forward(w):
        src, full = weights[w]
        size = src.shape[1]
        for k in zorder:
            block = rows(full, zp(-k) * ny + y, size)
            remote(block, block, wz_s.at[w, k - 1], wz_r.at[w, k - 1],
                   fdev(zp(k), y)).wait_recv()
            for j in range(1, ny):
                send(block, block, wy_s.at[w, k, j - 1], wy_r.at[w, k, j - 1], fdev(z, yp(j)))

    def weight_wait(w):
        src, full = weights[w]
        size = src.shape[1]
        locals_[w].wait()
        for k in [0] + zorder:
            for j in range(1, ny):
                block = rows(full, zp(-k) * ny + yp(-j), size)
                remote(block, block, wy_s.at[w, k, j - 1], wy_r.at[w, k, j - 1],
                       fdev(z, yp(j))).wait_recv()

    acts = ((tok_in, tok), (cot_in, cot))

    def act_start(w):
        src, full = acts[w]
        for k in range(1, nx):
            send(src, rows(full, e, T), tx_s.at[w, k - 1], tx_r.at[w, k - 1], edev(xp(k), c))
        send(src, rows(full, e, T), tc_s.at[w, 0], tc_r.at[w, 0], edev(x, 1 - c))

    def act_forward(w):
        src, full = acts[w]
        started = []
        for k in range(1, nx):
            block = rows(full, xp(-k) * 2 + c, T)
            remote(block, block, tx_s.at[w, k - 1], tx_r.at[w, k - 1],
                   edev(xp(k), c)).wait_recv()
            copy = remote(block, block, tc_s.at[w, k], tc_r.at[w, k], edev(x, 1 - c))
            copy.start()
            started.append(copy)
        return started

    def act_wait(w):
        src, full = acts[w]
        locals_[2 + w].wait()
        for k in range(nx):
            block = rows(full, xp(-k) * 2 + 1 - c, T)
            remote(block, block, tc_s.at[w, k], tc_r.at[w, k], edev(x, 1 - c)).wait_recv()

    weight_start(0)
    act_start(0)
    for i in range(1, ne):
        other = lax.rem(e + i, ne)
        send(gate_in.at[other], rows(gate, e, T), g_s.at[i - 1], g_r.at[i - 1], {"ep": other})
    act_start(1)
    tok_forwards = act_forward(0)
    weight_forward(0)
    weight_start(1)
    cot_forwards = act_forward(1)

    act_wait(1)
    for copy in cot_forwards:
        copy.wait_send()
    for i in range(1, ne):
        block = rows(gate, lax.rem(e - i + ne, ne), T)
        remote(block, block, g_s.at[i - 1], g_r.at[i - 1], {"ep": lax.rem(e + i, ne)}).wait_recv()

    @tiles(R, 16)
    def _(r):
        cot[r, :] = (cot[r, :].astype(F32) * gate[r, 0:1]).astype(BF16)

    act_wait(0)
    weight_wait(0)

    @tiles(FF, 256)
    def _(n):
        slope[:, n] = dot(tok[...], up[:, n], NN)

    @tiles(R, 16)
    def _(r):
        value, grad = gelu_parts(slope[r, :])
        hidden[r, :] = value.astype(BF16)
        slope[r, :] = grad

    @tiles(D, 512)
    def _(n):
        dpart[:, n] = dot(hidden[...], cot[:, n], TN).astype(BF16)

    parts = ((upart, ry_u, rz_u, ug_out), (dpart, ry_d, rz_d, dg_out))

    def part_start(w):
        part, ry, rz, out = parts[w]
        size = out.shape[1]
        for k in zorder + [0]:
            for j in range(1, ny):
                send(rows(part, zp(k) * ny + yp(j), size), ry.at[(j - 1) * nz + k],
                     ry_s.at[w, k, j - 1], ry_r.at[w, k, j - 1], fdev(z, yp(j)))

    def part_pair(w):
        part, ry, rz, out = parts[w]
        size = out.shape[1]
        for k in zorder + [0]:
            index = zp(k) * ny + y
            for j in range(1, ny):
                slot = ry.at[(j - 1) * nz + k]
                remote(slot, slot, ry_s.at[w, k, j - 1], ry_r.at[w, k, j - 1],
                       fdev(z, yp(j))).wait_recv()

            @tiles(size, 16)
            def _(r):
                at = pl.ds(pl.multiple_of(index * size + r.start, 16), 16)
                total = part[at, :].astype(F32)
                for j in range(1, ny):
                    total += ry[(j - 1) * nz + k, r, :].astype(F32)
                part[at, :] = total.astype(BF16)

            if k:
                send(rows(part, index, size), rz.at[k - 1], rz_s.at[w, k - 1],
                     rz_r.at[w, k - 1], fdev(zp(k), y))

    def part_end(w):
        part, ry, rz, out = parts[w]
        size = out.shape[1]
        for k in zorder:
            slot = rz.at[k - 1]
            remote(slot, slot, rz_s.at[w, k - 1], rz_r.at[w, k - 1], fdev(zp(k), y)).wait_recv()

        @tiles(size, 16)
        def _(r):
            at = pl.ds(pl.multiple_of(f * size + r.start, 16), 16)
            total = part[at, :].astype(F32)
            for k in zorder:
                total += rz[k - 1, r, :].astype(F32)
            out[0, r, :] = total.astype(BF16)

    backs = ((cot, rc_m, rx_m, mixed_out), (tok, rc_t, rx_t, tg_out))

    def back_start(w):
        full, rc, rx, out = backs[w]
        for k in range(nx):
            k = (k + 1) % nx
            send(rows(full, xp(k) * 2 + 1 - c, T), rc.at[k], rc_s.at[w, k], rc_r.at[w, k],
                 edev(x, 1 - c))

    def back_pair(w):
        full, rc, rx, out = backs[w]
        for k in range(nx):
            k = (k + 1) % nx
            index = xp(k) * 2 + c
            slot = rc.at[k]
            remote(slot, slot, rc_s.at[w, k], rc_r.at[w, k], edev(x, 1 - c)).wait_recv()

            @tiles(T, 16)
            def _(r):
                at = pl.ds(pl.multiple_of(index * T + r.start, 16), 16)
                full[at, :] = (full[at, :].astype(F32) + rc[k, r, :].astype(F32)).astype(BF16)

            if k:
                send(rows(full, index, T), rx.at[k - 1], rx_s.at[w, k - 1], rx_r.at[w, k - 1],
                     edev(xp(k), c))

    def back_end(w):
        full, rc, rx, out = backs[w]
        for k in range(1, nx):
            slot = rx.at[k - 1]
            remote(slot, slot, rx_s.at[w, k - 1], rx_r.at[w, k - 1], edev(xp(k), c)).wait_recv()

        @tiles(T, 16)
        def _(r):
            at = pl.ds(pl.multiple_of(e * T + r.start, 16), 16)
            total = full[at, :].astype(F32)
            for k in range(1, nx):
                total += rx[k - 1, r, :].astype(F32)
            out[r, :] = total.astype(BF16)

    part_start(1)
    weight_forward(1)
    weight_wait(1)

    @tiles(FF, 256)
    def _(n):
        dpre[:, n] = (dot(cot[...], down[n, :], NT) * slope[:, n]).astype(BF16)

    @tiles(D, 384)
    def _(n):
        upart[n, :] = dot(tok[:, n], dpre[...], TN).astype(BF16)

    part_start(0)

    @tiles(D, 512)
    def _(n):
        cot[:, n] = (dot(hidden[...], down[:, n], NN) * gate[:, 0:1]).astype(BF16)

    back_start(0)
    for copy in tok_forwards:
        copy.wait_send()

    @tiles(D, 512)
    def _(n):
        tok[:, n] = dot(dpre[...], up[n, :], NT).astype(BF16)

    back_start(1)
    part_pair(1)
    back_pair(0)
    back_pair(1)
    part_pair(0)
    part_end(1)
    back_end(0)
    back_end(1)
    part_end(0)
    for copy in sends:
        copy.wait_send()


def body(tokens, expert_ids, gates, up_weight, down_weight, cotangent):
    nf, ne = lax.axis_size("fsdp"), lax.axis_size("ep")
    nz = 4
    ny, nx = nf // nz, ne // 2
    T, D = tokens.shape
    R = ne * T
    su, FF = up_weight.shape[1:]
    sd = down_weight.shape[1]
    chosen = expert_ids[None] == jnp.arange(ne, dtype=jnp.int32)[:, None, None]
    dense = jnp.sum(jnp.where(chosen, gates[None], 0.0), axis=2)
    gcols = jnp.broadcast_to(dense[:, :, None], (ne, T, LANES))
    anyspace = pl.BlockSpec(memory_space=pl.ANY)
    vmem = pl.BlockSpec(memory_space=pltpu.VMEM)
    sem = pltpu.SemaphoreType.DMA
    V = pltpu.VMEM
    scratch = [
        V((D, FF), BF16), V((FF, D), BF16), V((R, D), BF16), V((R, D), BF16),
        V((R, LANES), F32), V((R, FF), F32), V((R, FF), BF16), V((R, FF), BF16),
        V((D, FF), BF16), V((FF, D), BF16),
        V(((ny - 1) * nz, su, FF), BF16), V(((ny - 1) * nz, sd, D), BF16),
        V((nz - 1, su, FF), BF16), V((nz - 1, sd, D), BF16),
        V((nx, T, D), BF16), V((nx, T, D), BF16),
        V((nx - 1, T, D), BF16), V((nx - 1, T, D), BF16),
        sem((4,)),
        sem((2, nz - 1)), sem((2, nz - 1)),
        sem((2, nz, ny - 1)), sem((2, nz, ny - 1)),
        sem((2, nx - 1)), sem((2, nx - 1)),
        sem((2, nx)), sem((2, nx)),
        sem((ne - 1,)), sem((ne - 1,)),
        sem((2, nz, ny - 1)), sem((2, nz, ny - 1)),
        sem((2, nz - 1)), sem((2, nz - 1)),
        sem((2, nx)), sem((2, nx)),
        sem((2, nx - 1)), sem((2, nx - 1)),
    ]
    return pl.pallas_call(
        functools.partial(kernel, nz, ny, nx),
        out_shape=(
            jax.ShapeDtypeStruct((T, D), BF16),
            jax.ShapeDtypeStruct((T, D), BF16),
            jax.ShapeDtypeStruct((1, su, FF), BF16),
            jax.ShapeDtypeStruct((1, sd, D), BF16),
        ),
        in_specs=[anyspace, anyspace, vmem, anyspace, anyspace],
        out_specs=(vmem, vmem, vmem, vmem),
        scratch_shapes=scratch,
        compiler_params=pltpu.CompilerParams(
            collective_id=0, has_side_effects=True, vmem_limit_bytes=63 * 1024 * 1024
        ),
    )(tokens, cotangent, gcols, up_weight, down_weight)


def solution(mesh):
    placed = (
        P(("fsdp", "ep"), None),
        P(("fsdp", "ep"), None),
        P(("fsdp", "ep"), None),
        P("ep", "fsdp", None),
        P("ep", "fsdp", None),
        P(("fsdp", "ep"), None),
    )
    return jax.shard_map(
        body,
        mesh=mesh,
        in_specs=placed,
        out_specs=(
            P(("fsdp", "ep"), None),
            P(("fsdp", "ep"), None),
            P("ep", "fsdp", None),
            P("ep", "fsdp", None),
        ),
        check_vma=False,
    )
```

time: 535 us -> 289 us (0.54)
  waiting for transfers between devices: 461 us -> 0 us
  Pallas kernels: 0 us -> 280 us
  matrix products: 37.8 us -> 0 us
  between operations: 14.2 us -> 0.65 us
  local copies, waits for them, and re-layouts: 14.3 us -> 6.42 us
  blocking collectives: 6.11 us -> 0 us
    pallas_call x0 -> x1, Pallas kernels: none -> 280 us  [body(): pl.pallas_call(functools.partial(kernel, nz, ny, nx), out_shape=(jax.Shap...]
    all_gather x4 -> x0, waiting for transfers between devices: 210 us -> none  [the longest x1 82.1 us: body(): up = lax.all_gather(up_weight, 'fsdp', axis=1, tiled=True)[0]]
    reduce_scatter x3 -> x0, waiting for transfers between devices: 179 us -> none  [the longest x1 99.7 us: body(): lax.psum_scatter(contract_first(hidden, grad_rows).astype(bf16), 'fsdp',...]
    unnamed x9 -> x0, waiting for transfers between devices: 72.4 us -> none
    dot_general x6 -> x0, matrix products: 37.8 us -> none  [the longest x2 13.4 us: contract_last(): lax.dot_general(left, right, (((1,), (1,)), ((), ())), preferred_element_...]
    unnamed x17 -> x10, local copies, waits for them, and re-layouts: 14.3 us -> 5.58 us
    all_gather x1 -> x0, blocking collectives: 6.11 us -> none  [body(): all_gates = lax.all_gather(dense_gates, 'ep', axis=0, tiled=True)]
  transfers between devices with their start and end apart: 8 -> 0, of which waited for: 8 -> 0; matrix products, arithmetic and copies ran while one was open for 5% -> 0% of each run, Pallas kernels for 0% -> 0%
where the time goes in v2:
time: 289 us; the launch traced here: 288 us
  Pallas kernels  280 us (97%)
  local copies, waits for them, and re-layouts  6.42 us (2%)
    pallas_call x1, Pallas kernels, body(): pl.pallas_call(functools.partial(kernel, nz, ny, nx), out_shape=(jax.Shap...  280 us

profile of v2, /device:TPU:0, one launch (start us, length us, event | category | flops | bytes accessed | tf_op | source)
XLA Modules:
  0.0 288.3 jit_solution(9475670114738001044)
XLA Ops:
  0.6 0.7 select_reduce_fusion
  1.3 0.8 broadcast_in_dim.23.gate_in
  2.2 280.5 %shard_map.93 = (bf16[128,3072]{1,0:T(8,128)(2,1)}, bf16[128,3072]{1,0:T(8,128)(2,1)}, bf16[1,384,768]{2,1,0:T(8,128)(2,1)}, bf16[1,96,3072]{2,1,0:T(8,128)(2,1)}) custom-call(bf16[128,3072]{1,0:T(8,128)(2,1)} %tok_in.1, bf16[128,3072]{1,0:T(8,128)(2,1)} %cot_in.1, f32[4,128,128]{2,1,0:T(8,128)} %broadcast_in_dim.23.gate_in, bf16[1,384,768]{2,1,0:T(8,128)(2,1)} %up_in.1, ...), custom_call_target="tpu_custom_call" | custom-call | tf_op jit(solution)/shard_map/pallas_call | solution.py:374
  282.7 0.0 copy-start
  282.7 2.1 copy.16
  284.8 0.0 copy-done
  284.8 0.0 copy-start.2
  284.8 0.9 copy.17
  285.7 0.5 copy-done.2
  286.2 0.0 copy-start.1
  286.2 0.8 copy.18
  287.0 0.5 copy-done.1
  287.4 0.8 copy.19
Async XLA Ops:
  282.7 2.1 copy-start
  284.8 1.3 copy-start.2
  286.2 1.3 copy-start.1

commit v3 on v2

--- a/solution.py
+++ b/solution.py
@@ -33,6 +33,10 @@
 TN = ((0,), (0,))
 
 
+def tail_rows(size):
+    return max(16, size // 6 // 16 * 16)
+
+
 def tiles(count, size):
     def run(fn):
         @pl.loop(0, count // size)
@@ -47,9 +51,10 @@
     tok_in, cot_in, gate_in, up_in, down_in,
     mixed_out, tg_out, ug_out, dg_out,
     up, down, tok, cot, gate, slope, hidden, dpre, upart, dpart,
-    ry_u, ry_d, rz_u, rz_d, rc_m, rc_t, rx_m, rx_t,
-    local_sem, wz_s, wz_r, wy_s, wy_r, tx_s, tx_r, tc_s, tc_r, g_s, g_r,
-    ry_s, ry_r, rz_s, rz_r, rc_s, rc_r, rx_s, rx_r,
+    ry_u, ry_d, rz_u, rz_d, rt_u, rt_d, ft_u, ft_d, rc_m, rc_t, rx_m, rx_t,
+    local_sem, wz_s, wz_r, wt_s, wt_r, wo_s, wo_r, wy_s, wy_r,
+    tx_s, tx_r, tc_s, tc_r, g_s, g_r,
+    ry_s, ry_r, rz_s, rz_r, rt_s, rt_r, ft_s, ft_r, rc_s, rc_r, rx_s, rx_r,
 ):
     ne = 2 * nx
     f = lax.axis_index("fsdp")
@@ -64,6 +69,9 @@
     def zp(k):
         return lax.rem(z + k + nz, nz)
 
+    def inside(zz):
+        return (zz >= 0) & (zz < nz)
+
     def yp(j):
         return lax.rem(y + j + ny, ny)
 
@@ -86,6 +94,16 @@
         )
 
     sends = []
+    guarded = []
+
+    def send_when(there, copies):
+        @pl.when(there)
+        def _():
+            for copy in copies:
+                copy.start()
+
+        guarded.append((there, copies))
+
 
     def send(src, dst, ss, rs, dev):
         copy = remote(src, dst, ss, rs, dev)
@@ -113,37 +131,84 @@
     pl.semaphore_wait(barrier, len(peers))
 
     weights = ((up_in, up), (down_in, down))
-    zorder = [1, nz - 1] + list(range(2, nz - 1))
+
+    def span(ref, index, size, begin, count):
+        return ref.at[pl.ds(pl.multiple_of(index * size + begin, 16), count)]
+
+    def chain(w, sgn, b, src=None):
+        full = weights[w][1]
+        size = weights[w][0].shape[1]
+        block = rows(full, b * ny + y, size)
+        way = (1 - sgn) // 2
+        return remote(block if src is None else src, block, wz_s.at[w, way, b],
+                      wz_r.at[w, way, b], fdev(zp(sgn), y))
+
+    def chain_tail(w, sgn, b, j):
+        full = weights[w][1]
+        size = weights[w][0].shape[1]
+        q = tail_rows(size)
+        block = span(full, b * ny + yp(-j), size, size - q, q)
+        way = (1 - sgn) // 2
+        return remote(block, block, wt_s.at[w, way, b, j - 1], wt_r.at[w, way, b, j - 1],
+                      fdev(zp(sgn), y))
+
+    def across(w, b, yy, j):
+        full = weights[w][1]
+        size = weights[w][0].shape[1]
+        block = span(full, b * ny + yy, size, 0, size - tail_rows(size))
+        return remote(block, block, wy_s.at[w, b, j - 1], wy_r.at[w, b, j - 1], fdev(z, yp(j)))
+
+    def own_across(w, yy, j, src=None):
+        full = weights[w][1]
+        size = weights[w][0].shape[1]
+        block = rows(full, z * ny + yy, size)
+        return remote(block if src is None else src, block, wo_s.at[w, j - 1], wo_r.at[w, j - 1],
+                      fdev(z, yp(j)))
 
     def weight_start(w):
-        src, full = weights[w]
-        size = src.shape[1]
-        for k in zorder:
-            send(src.at[0], rows(full, f, size), wz_s.at[w, k - 1], wz_r.at[w, k - 1],
-                 fdev(zp(k), y))
+        src = weights[w][0].at[0]
+        for sgn in (1, -1):
+            send_when(inside(z + sgn), [chain(w, sgn, z, src)])
         for j in range(1, ny):
-            send(src.at[0], rows(full, f, size), wy_s.at[w, 0, j - 1], wy_r.at[w, 0, j - 1],
-                 fdev(z, yp(j)))
-
-    def weight_forward(w):
-        src, full = weights[w]
-        size = src.shape[1]
-        for k in zorder:
-            block = rows(full, zp(-k) * ny + y, size)
-            remote(block, block, wz_s.at[w, k - 1], wz_r.at[w, k - 1],
-                   fdev(zp(k), y)).wait_recv()
+            copy = own_across(w, y, j, src)
+            copy.start()
+            sends.append(copy)
+
+    def tail_start(w):
+        for j in range(1, ny):
+            own_across(w, yp(-j), j).wait_recv()
+        for sgn in (1, -1):
+            send_when(inside(z + sgn), [chain_tail(w, sgn, z, j) for j in range(1, ny)])
+
+    def hop(w, s):
+        for sgn in (1, -1):
+            b = zp(-sgn * s)
+            there = inside(z - sgn * s)
+
+            @pl.when(there)
+            def _():
+                chain(w, sgn, b).wait_recv()
+
+            send_when(there & inside(z + sgn), [chain(w, sgn, b)])
+            send_when(there, [across(w, b, y, j) for j in range(1, ny)])
+
+    def hop_tail(w, s):
+        for sgn in (1, -1):
+            b = zp(-sgn * s)
+            there = inside(z - sgn * s)
+
+            @pl.when(there)
+            def _():
+                for j in range(1, ny):
+                    chain_tail(w, sgn, b, j).wait_recv()
+
+            send_when(there & inside(z + sgn), [chain_tail(w, sgn, b, j) for j in range(1, ny)])
+
+    def weight_wait(w):
+        locals_[w].wait()
+        for k in range(1, nz):
             for j in range(1, ny):
-                send(block, block, wy_s.at[w, k, j - 1], wy_r.at[w, k, j - 1], fdev(z, yp(j)))
-
-    def weight_wait(w):
-        src, full = weights[w]
-        size = src.shape[1]
-        locals_[w].wait()
-        for k in [0] + zorder:
-            for j in range(1, ny):
-                block = rows(full, zp(-k) * ny + yp(-j), size)
-                remote(block, block, wy_s.at[w, k, j - 1], wy_r.at[w, k, j - 1],
-                       fdev(z, yp(j))).wait_recv()
+                across(w, zp(k), yp(-j), j).wait_recv()
 
     acts = ((tok_in, tok), (cot_in, cot))
 
@@ -178,9 +243,15 @@
         other = lax.rem(e + i, ne)
         send(gate_in.at[other], rows(gate, e, T), g_s.at[i - 1], g_r.at[i - 1], {"ep": other})
     act_start(1)
+    hop(0, 1)
     tok_forwards = act_forward(0)
-    weight_forward(0)
+    tail_start(0)
+    hop(0, 2)
+    hop_tail(0, 1)
+    hop(0, 3)
     weight_start(1)
+    hop_tail(0, 2)
+    hop_tail(0, 3)
     cot_forwards = act_forward(1)
 
     act_wait(1)
@@ -195,11 +266,16 @@
         cot[r, :] = (cot[r, :].astype(F32) * gate[r, 0:1]).astype(BF16)
 
     act_wait(0)
+    hop(1, 1)
+    tail_start(1)
     weight_wait(0)
 
     @tiles(FF, 256)
     def _(n):
         slope[:, n] = dot(tok[...], up[:, n], NN)
+
+    hop(1, 2)
+    hop_tail(1, 1)
 
     @tiles(R, 16)
     def _(r):
@@ -211,52 +287,125 @@
     def _(n):
         dpart[:, n] = dot(hidden[...], cot[:, n], TN).astype(BF16)
 
-    parts = ((upart, ry_u, rz_u, ug_out), (dpart, ry_d, rz_d, dg_out))
+    parts = ((upart, ry_u, rz_u, rt_u, ft_u, ug_out), (dpart, ry_d, rz_d, rt_d, ft_d, dg_out))
+
+    flip = lax.div(z, 2)
+    near = z + flip * (3 - 2 * z)
+    order = [d + flip * (3 - 2 * d) for d in (near * 0 + 3, 2 - 2 * near, 1 + near, near)]
+
+    def give(w, d, yy, j):
+        part, ry = parts[w][:2]
+        size = parts[w][-1].shape[1]
+        return remote(span(part, d * ny + yy, size, 0, size - tail_rows(size)),
+                      ry.at[(j - 1) * nz + d], ry_s.at[w, d, j - 1], ry_r.at[w, d, j - 1],
+                      fdev(z, yp(j)))
+
+    def run_block(w, way, d, nxt):
+        part, ry, rz = parts[w][:3]
+        size = parts[w][-1].shape[1]
+        return remote(rows(part, d * ny + y, size), rz.at[way, d], rz_s.at[w, d],
+                      rz_r.at[w, way, d], fdev(nxt, y))
+
+    def run_tail(w, way, d, nxt, j):
+        part, rt = parts[w][0], parts[w][3]
+        size = parts[w][-1].shape[1]
+        q = tail_rows(size)
+        return remote(span(part, d * ny + yp(j), size, size - q, q), rt.at[way, d, j - 1],
+                      rt_s.at[w, d, j - 1], rt_r.at[w, way, d, j - 1], fdev(nxt, y))
+
+    def last_tail(w, j):
+        part, ft = parts[w][0], parts[w][4]
+        size = parts[w][-1].shape[1]
+        q = tail_rows(size)
+        return remote(span(part, z * ny + yp(j), size, size - q, q), ft.at[j - 1],
+                      ft_s.at[w, j - 1], ft_r.at[w, j - 1], fdev(z, yp(j)))
 
     def part_start(w):
-        part, ry, rz, out = parts[w]
+        for d in order:
+            for j in range(1, ny):
+                copy = give(w, d, yp(j), j)
+                copy.start()
+                sends.append(copy)
+
+    def add(part, start, count, others):
+        @tiles(count, 16)
+        def _(r):
+            at = pl.ds(pl.multiple_of(start + r.start, 16), 16)
+            total = part[at, :].astype(F32)
+            for other in others:
+                total += other[r, :].astype(F32)
+            part[at, :] = total.astype(BF16)
+
+    def pair(w, d):
+        part, ry = parts[w][:2]
+        size = parts[w][-1].shape[1]
+        for j in range(1, ny):
+            give(w, d, y, j).wait_recv()
+        add(part, (d * ny + y) * size, size - tail_rows(size),
+            [ry.at[(j - 1) * nz + d] for j in range(1, ny)])
+
+    def run(w, p):
+        part, ry, rz, rt = parts[w][:4]
+        size = parts[w][-1].shape[1]
+        q = tail_rows(size)
+        d = order[p]
+        way = jnp.where(d > z, 0, 1)
+        sgn = 1 - 2 * way
+        nxt = z + sgn
+        pair(w, d)
+
+        @pl.when(inside(z - sgn))
+        def _():
+            run_block(w, way, d, nxt).wait_recv()
+            for j in range(1, ny):
+                run_tail(w, way, d, nxt, j).wait_recv()
+            add(part, (d * ny + y) * size, size, [rz.at[way, d]])
+            for j in range(1, ny):
+                add(part, (d * ny + yp(j)) * size + size - q, q, [rt.at[way, d, j - 1]])
+
+        copies = [run_block(w, way, d, nxt)]
+        copies += [run_tail(w, way, d, nxt, j) for j in range(1, ny)]
+        for copy in copies:
+            copy.start()
+            sends.append(copy)
+
+    def part_last(w):
+        part, ry, rz, rt = parts[w][:4]
+        size = parts[w][-1].shape[1]
+        q = tail_rows(size)
+        pair(w, z)
+        for way in range(2):
+            sgn = 1 - 2 * way
+
+            @pl.when(inside(z - sgn))
+            def _():
+                for j in range(1, ny):
+                    run_tail(w, way, z, zp(1), j).wait_recv()
+                    add(part, (z * ny + yp(j)) * size + size - q, q, [rt.at[way, z, j - 1]])
+
+        for j in range(1, ny):
+            copy = last_tail(w, j)
+            copy.start()
+            sends.append(copy)
+        for way in range(2):
+            sgn = 1 - 2 * way
+
+            @pl.when(inside(z - sgn))
+            def _():
+                run_block(w, way, z, zp(1)).wait_recv()
+                add(part, (z * ny + y) * size, size, [rz.at[way, z]])
+
+    def part_end(w):
+        part, ry, rz, rt, ft, out = parts[w]
         size = out.shape[1]
-        for k in zorder + [0]:
-            for j in range(1, ny):
-                send(rows(part, zp(k) * ny + yp(j), size), ry.at[(j - 1) * nz + k],
-                     ry_s.at[w, k, j - 1], ry_r.at[w, k, j - 1], fdev(z, yp(j)))
-
-    def part_pair(w):
-        part, ry, rz, out = parts[w]
-        size = out.shape[1]
-        for k in zorder + [0]:
-            index = zp(k) * ny + y
-            for j in range(1, ny):
-                slot = ry.at[(j - 1) * nz + k]
-                remote(slot, slot, ry_s.at[w, k, j - 1], ry_r.at[w, k, j - 1],
-                       fdev(z, yp(j))).wait_recv()
-
-            @tiles(size, 16)
-            def _(r):
-                at = pl.ds(pl.multiple_of(index * size + r.start, 16), 16)
-                total = part[at, :].astype(F32)
-                for j in range(1, ny):
-                    total += ry[(j - 1) * nz + k, r, :].astype(F32)
-                part[at, :] = total.astype(BF16)
-
-            if k:
-                send(rows(part, index, size), rz.at[k - 1], rz_s.at[w, k - 1],
-                     rz_r.at[w, k - 1], fdev(zp(k), y))
-
-    def part_end(w):
-        part, ry, rz, out = parts[w]
-        size = out.shape[1]
-        for k in zorder:
-            slot = rz.at[k - 1]
-            remote(slot, slot, rz_s.at[w, k - 1], rz_r.at[w, k - 1], fdev(zp(k), y)).wait_recv()
+        q = tail_rows(size)
+        for j in range(1, ny):
+            last_tail(w, j).wait_recv()
+        add(part, (z * ny + y) * size + size - q, q, [ft.at[j - 1] for j in range(1, ny)])
 
         @tiles(size, 16)
         def _(r):
-            at = pl.ds(pl.multiple_of(f * size + r.start, 16), 16)
-            total = part[at, :].astype(F32)
-            for k in zorder:
-                total += rz[k - 1, r, :].astype(F32)
-            out[0, r, :] = total.astype(BF16)
+            out[0, r, :] = part[pl.ds(pl.multiple_of(f * size + r.start, 16), 16), :]
 
     backs = ((cot, rc_m, rx_m, mixed_out), (tok, rc_t, rx_t, tg_out))
 
@@ -298,25 +447,31 @@
                 total += rx[k - 1, r, :].astype(F32)
             out[r, :] = total.astype(BF16)
 
+    hop(1, 3)
+    hop_tail(1, 2)
     part_start(1)
-    weight_forward(1)
+    hop_tail(1, 3)
     weight_wait(1)
 
     @tiles(FF, 256)
     def _(n):
         dpre[:, n] = (dot(cot[...], down[n, :], NT) * slope[:, n]).astype(BF16)
 
+    run(1, 0)
+
     @tiles(D, 384)
     def _(n):
         upart[n, :] = dot(tok[:, n], dpre[...], TN).astype(BF16)
 
     part_start(0)
+    run(1, 1)
 
     @tiles(D, 512)
     def _(n):
         cot[:, n] = (dot(hidden[...], down[:, n], NN) * gate[:, 0:1]).astype(BF16)
 
     back_start(0)
+    run(1, 2)
     for copy in tok_forwards:
         copy.wait_send()
 
@@ -325,16 +480,24 @@
         tok[:, n] = dot(dpre[...], up[n, :], NT).astype(BF16)
 
     back_start(1)
-    part_pair(1)
     back_pair(0)
     back_pair(1)
-    part_pair(0)
+    run(0, 0)
+    part_last(1)
+    back_end(0)
+    run(0, 1)
+    back_end(1)
     part_end(1)
-    back_end(0)
-    back_end(1)
+    run(0, 2)
+    part_last(0)
     part_end(0)
     for copy in sends:
         copy.wait_send()
+    for there, copies in guarded:
+        @pl.when(there)
+        def _():
+            for copy in copies:
+                copy.wait_send()
 
 
 def body(tokens, expert_ids, gates, up_weight, down_weight, cotangent):
@@ -348,6 +511,7 @@
     chosen = expert_ids[None] == jnp.arange(ne, dtype=jnp.int32)[:, None, None]
     dense = jnp.sum(jnp.where(chosen, gates[None], 0.0), axis=2)
     gcols = jnp.broadcast_to(dense[:, :, None], (ne, T, LANES))
+    qu, qd = (tail_rows(size) for size in (su, sd))
     anyspace = pl.BlockSpec(memory_space=pl.ANY)
     vmem = pl.BlockSpec(memory_space=pltpu.VMEM)
     sem = pltpu.SemaphoreType.DMA
@@ -356,18 +520,24 @@
         V((D, FF), BF16), V((FF, D), BF16), V((R, D), BF16), V((R, D), BF16),
         V((R, LANES), F32), V((R, FF), F32), V((R, FF), BF16), V((R, FF), BF16),
         V((D, FF), BF16), V((FF, D), BF16),
-        V(((ny - 1) * nz, su, FF), BF16), V(((ny - 1) * nz, sd, D), BF16),
-        V((nz - 1, su, FF), BF16), V((nz - 1, sd, D), BF16),
+        V(((ny - 1) * nz, su - qu, FF), BF16), V(((ny - 1) * nz, sd - qd, D), BF16),
+        V((2, nz, su, FF), BF16), V((2, nz, sd, D), BF16),
+        V((2, nz, ny - 1, qu, FF), BF16), V((2, nz, ny - 1, qd, D), BF16),
+        V((ny - 1, qu, FF), BF16), V((ny - 1, qd, D), BF16),
         V((nx, T, D), BF16), V((nx, T, D), BF16),
         V((nx - 1, T, D), BF16), V((nx - 1, T, D), BF16),
         sem((4,)),
-        sem((2, nz - 1)), sem((2, nz - 1)),
+        sem((2, 2, nz)), sem((2, 2, nz)),
+        sem((2, 2, nz, ny - 1)), sem((2, 2, nz, ny - 1)),
+        sem((2, ny - 1)), sem((2, ny - 1)),
         sem((2, nz, ny - 1)), sem((2, nz, ny - 1)),
         sem((2, nx - 1)), sem((2, nx - 1)),
         sem((2, nx)), sem((2, nx)),
         sem((ne - 1,)), sem((ne - 1,)),
         sem((2, nz, ny - 1)), sem((2, nz, ny - 1)),
-        sem((2, nz - 1)), sem((2, nz - 1)),
+        sem((2, nz)), sem((2, 2, nz)),
+        sem((2, nz, ny - 1)), sem((2, 2, nz, ny - 1)),
+        sem((2, ny - 1)), sem((2, ny - 1)),
         sem((2, nx)), sem((2, nx)),
         sem((2, nx - 1)), sem((2, nx - 1)),
     ]
@@ -383,7 +553,7 @@
         out_specs=(vmem, vmem, vmem, vmem),
         scratch_shapes=scratch,
         compiler_params=pltpu.CompilerParams(
-            collective_id=0, has_side_effects=True, vmem_limit_bytes=63 * 1024 * 1024
+            collective_id=0, has_side_effects=True, vmem_limit_bytes=64 * 1024 * 1024 - 262144
         ),
     )(tokens, cotangent, gcols, up_weight, down_weight)
 

time: 289 us -> 221 us (0.76)
  Pallas kernels: 280 us -> 210 us
    pallas_call x1, Pallas kernels: 280 us -> 210 us  [body(): pl.pallas_call(functools.partial(kernel, nz, ny, nx), out_shape=(jax.Shap...]
where the time goes in v3:
time: 221 us; the launch traced here: 218 us
  Pallas kernels  210 us (95%)
  local copies, waits for them, and re-layouts  6.42 us (3%)
    pallas_call x1, Pallas kernels, body(): pl.pallas_call(functools.partial(kernel, nz, ny, nx), out_shape=(jax.Shap...  210 us
    unnamed x10, local copies, waits for them, and re-layouts  5.58 us

profile of v3, /device:TPU:0, one launch (start us, length us, event | category | flops | bytes accessed | tf_op | source)
XLA Modules:
  0.0 217.5 jit_solution(17015670188734939416)
XLA Ops:
  0.6 0.7 select_reduce_fusion
  1.3 0.8 broadcast_in_dim.23.gate_in
  2.2 209.7 %shard_map.93 = (bf16[128,3072]{1,0:T(8,128)(2,1)}, bf16[128,3072]{1,0:T(8,128)(2,1)}, bf16[1,384,768]{2,1,0:T(8,128)(2,1)}, bf16[1,96,3072]{2,1,0:T(8,128)(2,1)}) custom-call(bf16[128,3072]{1,0:T(8,128)(2,1)} %tok_in.1, bf16[128,3072]{1,0:T(8,128)(2,1)} %cot_in.1, f32[4,128,128]{2,1,0:T(8,128)} %broadcast_in_dim.23.gate_in, bf16[1,384,768]{2,1,0:T(8,128)(2,1)} %up_in.1, ...), custom_call_target="tpu_custom_call" | custom-call | tf_op jit(solution)/shard_map/pallas_call | solution.py:544
  211.9 0.0 copy-start
  211.9 2.1 copy.16
  214.1 0.0 copy-done
  214.1 0.0 copy-start.2
  214.1 0.9 copy.17
  214.9 0.5 copy-done.2
  215.4 0.0 copy-start.1
  215.4 0.8 copy.18
  216.2 0.5 copy-done.1
  216.7 0.8 copy.19
Async XLA Ops:
  211.9 2.1 copy-start
  214.1 1.3 copy-start.2
  215.4 1.3 copy-start.1
